TPU v7x, 512 devices: a whole 4x8x8 slice. The times are simulated.
512 devices in a mesh: leaf: 128 (over z, y, core), rhs: 4 (over x).
Axes of the slice: x: 4, y: 8, z: 8, core: 2. Of those that a mesh axis runs over, the one named last changes fastest.
Arguments:
- potential: float32 [128, 1048576], P('rhs', 'leaf'), may hold values from -6 to 6
- geometry: float32 [4, 1048576], P(None, 'leaf'), as said below
- near_count: int32 [4096], P('leaf'), may hold values from 3 to 12, as said below
- near_offset: int32 [4096, 12], P('leaf'), may hold values from -6 to 6, as said below
- far_offset: int32 [4096, 4], P('leaf'), may hold values from -8 to 8, as said below
- col_basis: bfloat16 [4096, 256, 64], P('leaf'), may hold values from -0.375 to 0.375
- row_basis: bfloat16 [4096, 256, 64], P('leaf'), may hold values from -0.5 to 0.5
- leaf_up: bfloat16 [4096, 64, 64], P('leaf'), may hold values from -0.125 to 0.125
- leaf_down: bfloat16 [4096, 64, 64], P('leaf'), may hold values from -0.75 to 0.75
- leaf_coupling: bfloat16 [4096, 4, 64, 64], P('leaf'), may hold values from -0.375 to 0.375
- up_transfer: bfloat16 [2, 64, 64], replicated, may hold values from -0.5 to 0.5
- down_transfer: bfloat16 [2, 64, 64], replicated, may hold values from -0.75 to 0.75
- sibling_coupling: bfloat16 [2, 64, 64], replicated, may hold values from -0.375 to 0.375
Outputs:
- field: float32 [128, 1048576], P('rhs', 'leaf')
Inputs may be any that keep to these rules, and one draw needn't show every extreme that they name: `geometry`: rows 0 to 2 are panel centroids, row 3 panel areas between 0.005 and 0.05. Each leaf cluster uses slots 0 to near_count - 1; some cluster uses all 12. `near_offset`: slot 0 of every cluster is the cluster itself (offset 0), slot 1 holds a positive offset and slot 2 a negative one; the other slots of a cluster hold distinct nonzero offsets. `far_offset`: every offset has magnitude above 6; the offsets of one cluster are distinct.
All inputs are finite; a program needn't handle non-finite values.
Results may differ from a plain program's by a relative error of at most 0.007.
Values may be sent and summed in bfloat16 or wider, within the bound.
No kernel may reach another device: no remote copies, remote signals or barrier semaphores. Data moves between devices by JAX's collectives and lax.ppermute only.
A program may use at most 64 MiB of HBM per device.

v0:
```python
import math
import jax
import jax.numpy as jnp
from jax import lax
from jax.sharding import PartitionSpec as P

NNEAR = 12
NWIN = 6
FWIN = 8


def with_halo(value, sides, width):
    for axis, dim in sides:
        devices, length = (lax.axis_size(axis), value.shape[dim])
        up = [(i, (i + 1) % devices) for i in range(devices - 1)]
        down = [(j, i) for i, j in up]
        last = lax.slice_in_dim(value, length - width, length, axis=dim)
        first = lax.slice_in_dim(value, 0, width, axis=dim)
        before = lax.ppermute(last, axis, up)
        after = lax.ppermute(first, axis, down)
        value = jnp.concatenate([before, value, after], axis=dim)
    return value


def from_partner(value, axis, apart):
    return lax.ppermute(value, axis, [(i, i ^ 1 << apart) for i in range(lax.axis_size(axis))])


def kernel_entries(target_geometry, source_geometry):
    squared = (target_geometry[0][:, :, None] - source_geometry[0][:, None, :]) ** 2
    squared = squared + (target_geometry[1][:, :, None] - source_geometry[1][:, None, :]) ** 2
    squared = squared + (target_geometry[2][:, :, None] - source_geometry[2][:, None, :]) ** 2
    spread = (target_geometry[3][:, :, None] + source_geometry[3][:, None, :]) / math.pi
    return source_geometry[3][:, None, :] / jnp.sqrt(squared + spread)


def select_side(table, side_bit):
    return lax.dynamic_index_in_dim(table, side_bit, 0, keepdims=False)


def per_device(
    potential,
    geometry,
    near_count,
    near_offset,
    far_offset,
    col_basis,
    row_basis,
    leaf_up,
    leaf_down,
    leaf_coupling,
    up_transfer,
    down_transfer,
    sibling_coupling,
):
    rows_here = potential.shape[0]
    clusters = near_count.shape[0]
    panels = col_basis.shape[1]
    basis_rank = col_basis.shape[2]
    partners_count = far_offset.shape[1]
    column_parts = lax.axis_size("rhs")
    per_part = clusters // column_parts
    first_local = lax.axis_index("rhs") * per_part
    window_width = per_part + 2 * NWIN
    stacked = jnp.concatenate([potential, geometry], axis=0)
    extended = with_halo(stacked, (("leaf", 1),), NWIN * panels)
    wide_rows = extended.shape[1] // panels
    value_rows = extended[:rows_here].astype(jnp.bfloat16)
    sources = lax.all_gather(value_rows, "rhs", axis=0, tiled=True)
    sources = sources.reshape(rows_here * column_parts, wide_rows, panels)
    all_rows = sources.shape[0]
    wide_geometry = extended[rows_here:].reshape(4, wide_rows, panels)
    local_geometry = lax.dynamic_slice_in_dim(wide_geometry, first_local, window_width, 1)
    target_geometry = local_geometry[:, NWIN : NWIN + per_part]
    live_counts = lax.dynamic_slice_in_dim(near_count, first_local, per_part, 0)
    offsets = lax.dynamic_slice_in_dim(near_offset, first_local, per_part, 0)
    own_clusters = NWIN + jnp.arange(per_part, dtype=jnp.int32)

    def add_slot(slot_index, running):
        shift_now = lax.dynamic_index_in_dim(offsets, slot_index, 1, keepdims=False)
        window_index = own_clusters + shift_now
        source_geometry = jnp.take(local_geometry, window_index, axis=1)
        source_values = jnp.take(sources, window_index + first_local, axis=1)
        live_mask = (slot_index < live_counts).astype(jnp.float32)
        near_block = (
            kernel_entries(target_geometry, source_geometry) * live_mask[:, None, None]
        ).astype(jnp.bfloat16)
        return running + jnp.einsum(
            "rcs,cts->rct", source_values, near_block, preferred_element_type=jnp.float32
        )

    start_sum = jnp.zeros((all_rows, per_part, panels), jnp.float32)
    near_part = lax.fori_loop(0, NNEAR, add_slot, start_sum)
    near_field = lax.all_to_all(
        near_part.reshape(all_rows, per_part * panels).astype(jnp.bfloat16),
        "rhs",
        split_axis=0,
        concat_axis=1,
        tiled=True,
    ).astype(jnp.float32)
    own_values = potential.astype(jnp.bfloat16).reshape(rows_here, clusters, panels)
    coefficients = jnp.einsum(
        "rcp,cpk->rck", own_values, col_basis, preferred_element_type=jnp.float32
    ).astype(jnp.bfloat16)
    rim_coefs = with_halo(
        coefficients.reshape(rows_here, clusters * basis_rank), (("leaf", 1),), FWIN * basis_rank
    )
    rim_coefs = rim_coefs.reshape(rows_here, clusters + 2 * FWIN, basis_rank)
    partner_index = jnp.arange(clusters, dtype=jnp.int32)[:, None] + FWIN + far_offset
    partners = jnp.take(rim_coefs, partner_index.reshape(-1), axis=1).reshape(
        rows_here, clusters, partners_count, basis_rank
    )
    leaf_far = jnp.einsum(
        "rcmk,cmkj->rcj", partners, leaf_coupling, preferred_element_type=jnp.float32
    )
    device_coef = jnp.einsum(
        "rck,ckj->rj", coefficients, leaf_up, preferred_element_type=jnp.float32
    ).astype(jnp.bfloat16)
    levels = lax.axis_size("leaf").bit_length() - 1
    device_index = lax.axis_index("leaf")
    couplings = []
    side_bits = []
    current = device_coef
    for tree_level in range(levels):
        side_bit = device_index // 2**tree_level % 2
        sibling = from_partner(current, "leaf", tree_level)
        couplings.append(
            jnp.dot(
                sibling, select_side(sibling_coupling, side_bit), preferred_element_type=jnp.float32
            )
        )
        side_bits.append(side_bit)
        if tree_level + 1 < levels:
            upward = jnp.dot(
                current, select_side(up_transfer, side_bit), preferred_element_type=jnp.float32
            )
            upward = upward + jnp.dot(
                sibling, select_side(up_transfer, 1 - side_bit), preferred_element_type=jnp.float32
            )
            current = upward.astype(jnp.bfloat16)
    local_sum = jnp.zeros((rows_here, basis_rank), jnp.float32)
    for tree_level in reversed(range(levels)):
        step_down = select_side(down_transfer, side_bits[tree_level]).astype(jnp.float32)
        local_sum = couplings[tree_level] + jnp.dot(
            local_sum, step_down, precision=lax.Precision.HIGHEST
        )
    leaf_local = leaf_far + jnp.einsum(
        "rk,ckj->rcj", local_sum, leaf_down.astype(jnp.float32), precision=lax.Precision.HIGHEST
    )
    leaf_local = leaf_local.astype(jnp.bfloat16)
    far_field = jnp.einsum(
        "rck,cpk->rcp", leaf_local, row_basis, preferred_element_type=jnp.float32
    )
    return near_field + far_field.reshape(rows_here, clusters * panels)


def solution(mesh):
    placed = (
        P("rhs", "leaf"),
        P(None, "leaf"),
        P("leaf"),
        P("leaf", None),
        P("leaf", None),
        P("leaf", None, None),
        P("leaf", None, None),
        P("leaf", None, None),
        P("leaf", None, None),
        P("leaf", None, None, None),
        P(),
        P(),
        P(),
    )
    return jax.shard_map(
        per_device, mesh=mesh, in_specs=placed, out_specs=P("rhs", "leaf"), check_vma=False
    )
```

profile of v0, /device:TPU:1, one launch (start us, length us, event | category | flops | bytes accessed | tf_op | source)
XLA Modules:
  0.0 244.2 jit_solution(15858377557532260188)
XLA Ops:
  9.3 8.8 %collective-permute-start.4 = (bf16[32,64]{1,0:T(8,128)(2,1)S(1)}, bf16[32,64]{1,0:T(8,128)(2,1)S(1)}, u32[]{:S(2)}, u32[]{:S(2)}) collective-permute-start(bf16[32,64]{1,0:T(8,128)(2,1)S(1)} %fusion.23), channel_id=1, source_target_pairs={{0,4},{4,0},{8,12},{12,8},{16,20},{20,16},{24,28},{28,24},{32,36},... | collective-permute-start | bytes 12296 | tf_op jit(solution)/shard_map/ppermute | solution.py:26
  18.9 1.9 reshape.114
  22.2 1.9 collective-permute-start.2
  24.1 3.0 %collective-permute-start.3 = (bf16[32,512]{1,0:T(8,128)(2,1)}, bf16[32,512]{1,0:T(8,128)(2,1)}, u32[]{:S(2)}, u32[]{:S(2)}) collective-permute-start(bf16[32,512]{1,0:T(8,128)(2,1)} %get-tuple-element.251), channel_id=1, source_target_pairs={{4,0},{8,4},{12,8},{16,12},{20,16},{24,20},{28,24},{32,28},{36,32}... | collective-permute-start | bytes 98312 | tf_op jit(solution)/shard_map/ppermute | solution.py:20
  28.8 2.5 %collective-permute-start = (f32[36,1536]{1,0:T(8,128)}, f32[36,1536]{1,0:T(8,128)}, u32[]{:S(2)}, u32[]{:S(2)}) collective-permute-start(f32[36,1536]{1,0:T(8,128)} %get-tuple-element.246), channel_id=1, source_target_pairs={{0,4},{4,8},{8,12},{12,16},{16,20},{20,24},{24,28},{28,32},{32,36}... | collective-permute-start | bytes 663560 | tf_op jit(solution)/shard_map/ppermute | solution.py:19
  31.4 2.4 %collective-permute-start.1 = (f32[36,1536]{1,0:T(8,128)}, f32[36,1536]{1,0:T(8,128)}, u32[]{:S(2)}, u32[]{:S(2)}) collective-permute-start(f32[36,1536]{1,0:T(8,128)} %get-tuple-element.247), channel_id=1, source_target_pairs={{4,0},{8,4},{12,8},{16,12},{20,16},{24,20},{28,24},{32,28},{36,32}... | collective-permute-start | bytes 663560 | tf_op jit(solution)/shard_map/ppermute | solution.py:20
  36.3 1.9 collective-permute-start.5
  38.3 2.7 %collective-permute-done.5 = bf16[32,64]{1,0:T(8,128)(2,1)S(1)} collective-permute-done((bf16[32,64]{1,0:T(8,128)(2,1)S(1)}, bf16[32,64]{1,0:T(8,128)(2,1)S(1)}, u32[]{:S(2)}, u32[]{:S(2)}) %collective-permute-start.5) | collective-permute-done | bytes 4128 | tf_op jit(solution)/shard_map/ppermute | solution.py:26
  41.1 1.9 collective-permute-start.6
  43.2 3.2 %collective-permute-done.6 = bf16[32,64]{1,0:T(8,128)(2,1)S(1)} collective-permute-done((bf16[32,64]{1,0:T(8,128)(2,1)S(1)}, bf16[32,64]{1,0:T(8,128)(2,1)S(1)}, u32[]{:S(2)}, u32[]{:S(2)}) %collective-permute-start.6) | collective-permute-done | bytes 4128 | tf_op jit(solution)/shard_map/ppermute | solution.py:26
  46.6 2.4 collective-permute-start.7
  49.1 5.7 %collective-permute-done.7 = bf16[32,64]{1,0:T(8,128)(2,1)S(1)} collective-permute-done((bf16[32,64]{1,0:T(8,128)(2,1)S(1)}, bf16[32,64]{1,0:T(8,128)(2,1)S(1)}, u32[]{:S(2)}, u32[]{:S(2)}) %collective-permute-start.7) | collective-permute-done | bytes 4128 | tf_op jit(solution)/shard_map/ppermute | solution.py:26
  55.6 1.9 collective-permute-start.8
  58.4 2.4 pad_maximum_fusion
  60.8 2.4 slice.115
  64.1 5.0 %collective-permute-start.9 = (bf16[32,64]{1,0:T(8,128)(2,1)S(1)}, bf16[32,64]{1,0:T(8,128)(2,1)S(1)}, u32[]{:S(2)}, u32[]{:S(2)}) collective-permute-start(bf16[32,64]{1,0:T(8,128)(2,1)S(1)} %fusion.28), channel_id=1, source_target_pairs={{0,128},{4,132},{8,136},{12,140},{16,144},{20,148},{24,152},{28,15... | collective-permute-start | bytes 12296 | tf_op jit(solution)/shard_map/ppermute | solution.py:26
  70.3 8.3 %collective-permute-start.10 = (bf16[32,64]{1,0:T(8,128)(2,1)S(1)}, bf16[32,64]{1,0:T(8,128)(2,1)S(1)}, u32[]{:S(2)}, u32[]{:S(2)}) collective-permute-start(bf16[32,64]{1,0:T(8,128)(2,1)S(1)} %fusion.29), channel_id=1, source_target_pairs={{0,256},{4,260},{8,264},{12,268},{16,272},{20,276},{24,280},{28,28... | collective-permute-start | bytes 12296 | tf_op jit(solution)/shard_map/ppermute | solution.py:26
  86.8 2.1 convolution_bitcast_fusion.2
  91.8 21.3 %all-gather.2.cloned.1.call-done = bf16[128,11264]{1,0:T(8,128)(2,1)} async-done(((bf16[32,11264]{1,0:T(8,128)(2,1)}), bf16[128,11264]{1,0:T(8,128)(2,1)}) %all-gather.2.cloned.1.call-update) | async-done | bytes 2883600 | tf_op jit(solution)/shard_map/all_gather | solution.py:69
  113.1 4.6 %copy.43 = bf16[128,11264]{0,1:T(8,128)(2,1)} copy(bf16[128,11264]{1,0:T(8,128)(2,1)} %all-gather.2.cloned.1.call-done) | data formatting | bytes 5767168 | tf_op jit(solution)/shard_map/all_gather | solution.py:69
  117.6 4.6 %copy.45 = bf16[128,44,256]{2,0,1:T(8,128)(2,1)} copy(bf16[128,44,256]{0,2,1:T(8,128)(2,1)} %bitcast.197) | data formatting | bytes 5767168
  122.2 96.9 %while.14 = (s32[]{:T(128)}, f32[128,8,256]{0,2,1:T(8,128)}, s32[8,12]{0,1:T(8,128)}, f32[4,20,256]{2,0,1:T(4,128)S(1)}, f32[4,8,256]{2,1,0:T(8,128)S(1)}, /*ind...) while((s32[]{:T(128)}, f32[128,8,256]{0,2,1:T(8,128)}, ...), condition=%wide.region_1.2_spmd.clone, body=%wide.region_0.1_spmd.clone.sunk | while | flops 142354592 | bytes 4071995 | solution.py:93
  123.6 2.4 gather_fusion.1
  126.1 2.9 %fusion.174 = f32[128,8,256]{0,2,1:T(8,128)} fusion(f32[128,8,256]{0,2,1:T(8,128)} %get-tuple-element.342, f32[8]{0:T(128)S(1)} %compare_convert_fusion.2, f32[8,256]{1,0:T(8,128)S(1)} %get-tuple-element.316, f32[8,256]{1,0:T(8,128)S(1)} %get-tuple-element.320, f32[8,256]{1,0:T(8,128)S(1)} %get-tuple-element.321, ...), kind=kOutput, calls=%fused_computation.6.clone.1 | convolution fusion | flops 142344192 | bytes 2687017 | tf_op jit(solution)/shard_map/while/body/eval_jaxpr/rcs,cts->rct/dot_general | solution.py:88
  130.5 2.4 gather_fusion.1
  132.9 4.3 %fusion.174 = f32[128,8,256]{0,2,1:T(8,128)} fusion(f32[128,8,256]{0,2,1:T(8,128)} %get-tuple-element.342, f32[8]{0:T(128)S(1)} %compare_convert_fusion.2, f32[8,256]{1,0:T(8,128)S(1)} %get-tuple-element.316, f32[8,256]{1,0:T(8,128)S(1)} %get-tuple-element.320, f32[8,256]{1,0:T(8,128)S(1)} %get-tuple-element.321, ...), kind=kOutput, calls=%fused_computation.6.clone.1 | convolution fusion | flops 142344192 | bytes 2687017 | tf_op jit(solution)/shard_map/while/body/eval_jaxpr/rcs,cts->rct/dot_general | solution.py:88
  138.6 2.4 gather_fusion.1
  141.1 4.3 %fusion.174 = f32[128,8,256]{0,2,1:T(8,128)} fusion(f32[128,8,256]{0,2,1:T(8,128)} %get-tuple-element.342, f32[8]{0:T(128)S(1)} %compare_convert_fusion.2, f32[8,256]{1,0:T(8,128)S(1)} %get-tuple-element.316, f32[8,256]{1,0:T(8,128)S(1)} %get-tuple-element.320, f32[8,256]{1,0:T(8,128)S(1)} %get-tuple-element.321, ...), kind=kOutput, calls=%fused_computation.6.clone.1 | convolution fusion | flops 142344192 | bytes 2687017 | tf_op jit(solution)/shard_map/while/body/eval_jaxpr/rcs,cts->rct/dot_general | solution.py:88
  146.8 2.4 gather_fusion.1
  149.3 4.3 %fusion.174 = f32[128,8,256]{0,2,1:T(8,128)} fusion(f32[128,8,256]{0,2,1:T(8,128)} %get-tuple-element.342, f32[8]{0:T(128)S(1)} %compare_convert_fusion.2, f32[8,256]{1,0:T(8,128)S(1)} %get-tuple-element.316, f32[8,256]{1,0:T(8,128)S(1)} %get-tuple-element.320, f32[8,256]{1,0:T(8,128)S(1)} %get-tuple-element.321, ...), kind=kOutput, calls=%fused_computation.6.clone.1 | convolution fusion | flops 142344192 | bytes 2687017 | tf_op jit(solution)/shard_map/while/body/eval_jaxpr/rcs,cts->rct/dot_general | solution.py:88
  155.0 2.4 gather_fusion.1
  157.4 4.3 %fusion.174 = f32[128,8,256]{0,2,1:T(8,128)} fusion(f32[128,8,256]{0,2,1:T(8,128)} %get-tuple-element.342, f32[8]{0:T(128)S(1)} %compare_convert_fusion.2, f32[8,256]{1,0:T(8,128)S(1)} %get-tuple-element.316, f32[8,256]{1,0:T(8,128)S(1)} %get-tuple-element.320, f32[8,256]{1,0:T(8,128)S(1)} %get-tuple-element.321, ...), kind=kOutput, calls=%fused_computation.6.clone.1 | convolution fusion | flops 142344192 | bytes 2687017 | tf_op jit(solution)/shard_map/while/body/eval_jaxpr/rcs,cts->rct/dot_general | solution.py:88
  163.2 2.4 gather_fusion.1
  165.6 4.3 %fusion.174 = f32[128,8,256]{0,2,1:T(8,128)} fusion(f32[128,8,256]{0,2,1:T(8,128)} %get-tuple-element.342, f32[8]{0:T(128)S(1)} %compare_convert_fusion.2, f32[8,256]{1,0:T(8,128)S(1)} %get-tuple-element.316, f32[8,256]{1,0:T(8,128)S(1)} %get-tuple-element.320, f32[8,256]{1,0:T(8,128)S(1)} %get-tuple-element.321, ...), kind=kOutput, calls=%fused_computation.6.clone.1 | convolution fusion | flops 142344192 | bytes 2687017 | tf_op jit(solution)/shard_map/while/body/eval_jaxpr/rcs,cts->rct/dot_general | solution.py:88
  171.4 2.4 gather_fusion.1
  173.8 4.3 %fusion.174 = f32[128,8,256]{0,2,1:T(8,128)} fusion(f32[128,8,256]{0,2,1:T(8,128)} %get-tuple-element.342, f32[8]{0:T(128)S(1)} %compare_convert_fusion.2, f32[8,256]{1,0:T(8,128)S(1)} %get-tuple-element.316, f32[8,256]{1,0:T(8,128)S(1)} %get-tuple-element.320, f32[8,256]{1,0:T(8,128)S(1)} %get-tuple-element.321, ...), kind=kOutput, calls=%fused_computation.6.clone.1 | convolution fusion | flops 142344192 | bytes 2687017 | tf_op jit(solution)/shard_map/while/body/eval_jaxpr/rcs,cts->rct/dot_general | solution.py:88
  179.6 2.4 gather_fusion.1
  182.0 4.3 %fusion.174 = f32[128,8,256]{0,2,1:T(8,128)} fusion(f32[128,8,256]{0,2,1:T(8,128)} %get-tuple-element.342, f32[8]{0:T(128)S(1)} %compare_convert_fusion.2, f32[8,256]{1,0:T(8,128)S(1)} %get-tuple-element.316, f32[8,256]{1,0:T(8,128)S(1)} %get-tuple-element.320, f32[8,256]{1,0:T(8,128)S(1)} %get-tuple-element.321, ...), kind=kOutput, calls=%fused_computation.6.clone.1 | convolution fusion | flops 142344192 | bytes 2687017 | tf_op jit(solution)/shard_map/while/body/eval_jaxpr/rcs,cts->rct/dot_general | solution.py:88
  187.8 2.4 gather_fusion.1
  190.2 4.3 %fusion.174 = f32[128,8,256]{0,2,1:T(8,128)} fusion(f32[128,8,256]{0,2,1:T(8,128)} %get-tuple-element.342, f32[8]{0:T(128)S(1)} %compare_convert_fusion.2, f32[8,256]{1,0:T(8,128)S(1)} %get-tuple-element.316, f32[8,256]{1,0:T(8,128)S(1)} %get-tuple-element.320, f32[8,256]{1,0:T(8,128)S(1)} %get-tuple-element.321, ...), kind=kOutput, calls=%fused_computation.6.clone.1 | convolution fusion | flops 142344192 | bytes 2687017 | tf_op jit(solution)/shard_map/while/body/eval_jaxpr/rcs,cts->rct/dot_general | solution.py:88
  196.0 2.4 gather_fusion.1
  198.4 4.3 %fusion.174 = f32[128,8,256]{0,2,1:T(8,128)} fusion(f32[128,8,256]{0,2,1:T(8,128)} %get-tuple-element.342, f32[8]{0:T(128)S(1)} %compare_convert_fusion.2, f32[8,256]{1,0:T(8,128)S(1)} %get-tuple-element.316, f32[8,256]{1,0:T(8,128)S(1)} %get-tuple-element.320, f32[8,256]{1,0:T(8,128)S(1)} %get-tuple-element.321, ...), kind=kOutput, calls=%fused_computation.6.clone.1 | convolution fusion | flops 142344192 | bytes 2687017 | tf_op jit(solution)/shard_map/while/body/eval_jaxpr/rcs,cts->rct/dot_general | solution.py:88
  204.2 2.4 gather_fusion.1
  206.6 4.3 %fusion.174 = f32[128,8,256]{0,2,1:T(8,128)} fusion(f32[128,8,256]{0,2,1:T(8,128)} %get-tuple-element.342, f32[8]{0:T(128)S(1)} %compare_convert_fusion.2, f32[8,256]{1,0:T(8,128)S(1)} %get-tuple-element.316, f32[8,256]{1,0:T(8,128)S(1)} %get-tuple-element.320, f32[8,256]{1,0:T(8,128)S(1)} %get-tuple-element.321, ...), kind=kOutput, calls=%fused_computation.6.clone.1 | convolution fusion | flops 142344192 | bytes 2687017 | tf_op jit(solution)/shard_map/while/body/eval_jaxpr/rcs,cts->rct/dot_general | solution.py:88
  212.4 2.4 gather_fusion.1
  214.8 4.3 %fusion.174 = f32[128,8,256]{0,2,1:T(8,128)} fusion(f32[128,8,256]{0,2,1:T(8,128)} %get-tuple-element.342, f32[8]{0:T(128)S(1)} %compare_convert_fusion.2, f32[8,256]{1,0:T(8,128)S(1)} %get-tuple-element.316, f32[8,256]{1,0:T(8,128)S(1)} %get-tuple-element.320, f32[8,256]{1,0:T(8,128)S(1)} %get-tuple-element.321, ...), kind=kOutput, calls=%fused_computation.6.clone.1 | convolution fusion | flops 142344192 | bytes 2687017 | tf_op jit(solution)/shard_map/while/body/eval_jaxpr/rcs,cts->rct/dot_general | solution.py:88
  221.9 4.1 %all-to-all-start = ((bf16[4,32,2048]{2,1,0:T(8,128)(2,1)}), bf16[4,32,2048]{2,1,0:T(8,128)(2,1)}, u32[]{:S(2)}, u32[]{:S(2)}) async-start(bf16[4,32,2048]{2,1,0:T(8,128)(2,1)} %convert_element_type.77), calls=%async_computation | async-start | bytes 1048576 | tf_op jit(solution)/shard_map/all_to_all | solution.py:94
  229.1 6.0 %all-to-all-done = bf16[4,32,2048]{2,1,0:T(8,128)(2,1)} async-done(((bf16[4,32,2048]{2,1,0:T(8,128)(2,1)}), bf16[4,32,2048]{2,1,0:T(8,128)(2,1)}, u32[]{:S(2)}, u32[]{:S(2)}) %all-to-all-start) | async-done | bytes 524320 | tf_op jit(solution)/shard_map/all_to_all | solution.py:94
  (245 shorter events, 49.1 us)
Async XLA Ops:
  6.5 80.3 %copy-start = (bf16[32,4,64,64]{3,2,1,0:T(8,128)(2,1)S(1)}, bf16[32,4,64,64]{3,2,1,0:T(8,128)(2,1)}, u32[]{:S(2)}) copy-start(bf16[32,4,64,64]{3,2,1,0:T(8,128)(2,1)} %param.24) | copy-start | bytes 3145732
  6.5 106.5 %all-gather.2.cloned.1.call-start = ((), (), s32[]{:S(2)}) async-start(), calls=%async_computation.1 | async-start | bytes 3604480 | tf_op jit(solution)/shard_map/all_gather | solution.py:69
  6.5 2.0 copy-start.3
  6.5 2.4 copy-start.5
  9.0 25.0 %copy-start.13 = (s32[32,4]{0,1:T(4,128)S(1)}, s32[32,4]{0,1:T(4,128)}, u32[]{:S(2)}) copy-start(s32[32,4]{0,1:T(4,128)} %param.19) | copy-start | bytes 1540
  9.0 26.3 %copy-start.2 = (bf16[2,64,64]{2,1,0:T(8,128)(2,1)S(1)}, bf16[2,64,64]{2,1,0:T(8,128)(2,1)}, u32[]{:S(2)}) copy-start(bf16[2,64,64]{2,1,0:T(8,128)(2,1)} %param.25) | copy-start | bytes 49156
  9.0 26.4 %copy-start.6 = (bf16[2,64,64]{2,1,0:T(8,128)(2,1)S(1)}, bf16[2,64,64]{2,1,0:T(8,128)(2,1)}, u32[]{:S(2)}) copy-start(bf16[2,64,64]{2,1,0:T(8,128)(2,1)} %param.26) | copy-start | bytes 49156
  9.0 26.5 %copy-start.12 = (s32[32,12]{0,1:T(8,128)S(1)}, s32[32,12]{0,1:T(8,128)}, u32[]{:S(2)}) copy-start(s32[32,12]{0,1:T(8,128)} %param.18) | copy-start | bytes 4612
  9.3 26.9 %collective-permute-start.4 = (bf16[32,64]{1,0:T(8,128)(2,1)S(1)}, bf16[32,64]{1,0:T(8,128)(2,1)S(1)}, u32[]{:S(2)}, u32[]{:S(2)}) collective-permute-start(bf16[32,64]{1,0:T(8,128)(2,1)S(1)} %fusion.23), channel_id=1, source_target_pairs={{0,4},{4,0},{8,12},{12,8},{16,20},{20,16},{24,28},{28,24},{32,36},... | collective-permute-start | bytes 12296 | tf_op jit(solution)/shard_map/ppermute | solution.py:26
  22.2 62.5 %collective-permute-start.2 = (bf16[32,512]{1,0:T(8,128)(2,1)}, bf16[32,512]{1,0:T(8,128)(2,1)}, u32[]{:S(2)}, u32[]{:S(2)}) collective-permute-start(bf16[32,512]{1,0:T(8,128)(2,1)} %get-tuple-element.250), channel_id=1, source_target_pairs={{0,4},{4,8},{8,12},{12,16},{16,20},{20,24},{24,28},{28,32},{32,36}... | collective-permute-start | bytes 98312 | tf_op jit(solution)/shard_map/ppermute | solution.py:19
  24.1 60.6 %collective-permute-start.3 = (bf16[32,512]{1,0:T(8,128)(2,1)}, bf16[32,512]{1,0:T(8,128)(2,1)}, u32[]{:S(2)}, u32[]{:S(2)}) collective-permute-start(bf16[32,512]{1,0:T(8,128)(2,1)} %get-tuple-element.251), channel_id=1, source_target_pairs={{4,0},{8,4},{12,8},{16,12},{20,16},{24,20},{28,24},{32,28},{36,32}... | collective-permute-start | bytes 98312 | tf_op jit(solution)/shard_map/ppermute | solution.py:20
  28.8 29.5 %collective-permute-start = (f32[36,1536]{1,0:T(8,128)}, f32[36,1536]{1,0:T(8,128)}, u32[]{:S(2)}, u32[]{:S(2)}) collective-permute-start(f32[36,1536]{1,0:T(8,128)} %get-tuple-element.246), channel_id=1, source_target_pairs={{0,4},{4,8},{8,12},{12,16},{16,20},{20,24},{24,28},{28,32},{32,36}... | collective-permute-start | bytes 663560 | tf_op jit(solution)/shard_map/ppermute | solution.py:19
  31.4 27.0 %collective-permute-start.1 = (f32[36,1536]{1,0:T(8,128)}, f32[36,1536]{1,0:T(8,128)}, u32[]{:S(2)}, u32[]{:S(2)}) collective-permute-start(f32[36,1536]{1,0:T(8,128)} %get-tuple-element.247), channel_id=1, source_target_pairs={{4,0},{8,4},{12,8},{16,12},{20,16},{24,20},{28,24},{32,28},{36,32}... | collective-permute-start | bytes 663560 | tf_op jit(solution)/shard_map/ppermute | solution.py:20
  36.2 21.3 %copy-start.8 = (bf16[32,64]{1,0:T(8,128)(2,1)}, bf16[32,64]{1,0:T(8,128)(2,1)S(1)}, u32[]{:S(2)}) copy-start(bf16[32,64]{1,0:T(8,128)(2,1)S(1)} %collective-permute-done.4) | copy-start | bytes 12292
  36.3 4.7 %collective-permute-start.5 = (bf16[32,64]{1,0:T(8,128)(2,1)S(1)}, bf16[32,64]{1,0:T(8,128)(2,1)S(1)}, u32[]{:S(2)}, u32[]{:S(2)}) collective-permute-start(bf16[32,64]{1,0:T(8,128)(2,1)S(1)} %fusion.24), channel_id=1, source_target_pairs={{0,8},{4,12},{8,0},{12,4},{16,24},{20,28},{24,16},{28,20},{32,40},... | collective-permute-start | bytes 12296 | tf_op jit(solution)/shard_map/ppermute | solution.py:26
  41.1 5.3 %collective-permute-start.6 = (bf16[32,64]{1,0:T(8,128)(2,1)S(1)}, bf16[32,64]{1,0:T(8,128)(2,1)S(1)}, u32[]{:S(2)}, u32[]{:S(2)}) collective-permute-start(bf16[32,64]{1,0:T(8,128)(2,1)S(1)} %fusion.25), channel_id=1, source_target_pairs={{0,16},{4,20},{8,24},{12,28},{16,0},{20,4},{24,8},{28,12},{32,48},... | collective-permute-start | bytes 12296 | tf_op jit(solution)/shard_map/ppermute | solution.py:26
  46.6 8.3 %collective-permute-start.7 = (bf16[32,64]{1,0:T(8,128)(2,1)S(1)}, bf16[32,64]{1,0:T(8,128)(2,1)S(1)}, u32[]{:S(2)}, u32[]{:S(2)}) collective-permute-start(bf16[32,64]{1,0:T(8,128)(2,1)S(1)} %fusion.26), channel_id=1, source_target_pairs={{0,32},{4,36},{8,40},{12,44},{16,48},{20,52},{24,56},{28,60},{32,0... | collective-permute-start | bytes 12296 | tf_op jit(solution)/shard_map/ppermute | solution.py:26
  54.9 2.7 %copy-start.10 = (bf16[32,64]{1,0:T(8,128)(2,1)}, bf16[32,64]{1,0:T(8,128)(2,1)S(1)}, u32[]{:S(2)}) copy-start(bf16[32,64]{1,0:T(8,128)(2,1)S(1)} %collective-permute-done.7) | copy-start | bytes 12292
  55.6 7.6 %collective-permute-start.8 = (bf16[32,64]{1,0:T(8,128)(2,1)}, bf16[32,64]{1,0:T(8,128)(2,1)}, u32[]{:S(2)}, u32[]{:S(2)}) collective-permute-start(bf16[32,64]{1,0:T(8,128)(2,1)} %fusion.27), channel_id=1, source_target_pairs={{0,64},{4,68},{8,72},{12,76},{16,80},{20,84},{24,88},{28,92},{32,9... | collective-permute-start | bytes 12296 | tf_op jit(solution)/shard_map/ppermute | solution.py:26
  58.4 23.8 %copy-start.7 = (bf16[2,64,64]{2,1,0:T(8,128)(2,1)S(1)}, bf16[2,64,64]{2,1,0:T(8,128)(2,1)}, u32[]{:S(2)}) copy-start(bf16[2,64,64]{2,1,0:T(8,128)(2,1)} %param.27) | copy-start | bytes 49156
  60.8 22.9 %copy-start.11 = (bf16[32,64]{1,0:T(8,128)(2,1)S(1)}, bf16[32,64]{1,0:T(8,128)(2,1)}, u32[]{:S(2)}) copy-start(bf16[32,64]{1,0:T(8,128)(2,1)} %copy-done.10) | copy-start | bytes 12292
  60.8 23.7 %copy-start.9 = (bf16[32,64]{1,0:T(8,128)(2,1)S(1)}, bf16[32,64]{1,0:T(8,128)(2,1)}, u32[]{:S(2)}) copy-start(bf16[32,64]{1,0:T(8,128)(2,1)} %copy-done.8) | copy-start | bytes 12292
  60.8 23.9 %copy-start.4 = (bf16[32,2048]{1,0:T(8,128)(2,1)S(1)}, bf16[32,2048]{1,0:T(8,128)(2,1)}, u32[]{:S(2)}) copy-start(bf16[32,2048]{1,0:T(8,128)(2,1)} %reshape.114) | copy-start | bytes 393220
  64.1 6.1 %collective-permute-start.9 = (bf16[32,64]{1,0:T(8,128)(2,1)S(1)}, bf16[32,64]{1,0:T(8,128)(2,1)S(1)}, u32[]{:S(2)}, u32[]{:S(2)}) collective-permute-start(bf16[32,64]{1,0:T(8,128)(2,1)S(1)} %fusion.28), channel_id=1, source_target_pairs={{0,128},{4,132},{8,136},{12,140},{16,144},{20,148},{24,152},{28,15... | collective-permute-start | bytes 12296 | tf_op jit(solution)/shard_map/ppermute | solution.py:26
  70.3 11.9 %collective-permute-start.10 = (bf16[32,64]{1,0:T(8,128)(2,1)S(1)}, bf16[32,64]{1,0:T(8,128)(2,1)S(1)}, u32[]{:S(2)}, u32[]{:S(2)}) collective-permute-start(bf16[32,64]{1,0:T(8,128)(2,1)S(1)} %fusion.29), channel_id=1, source_target_pairs={{0,256},{4,260},{8,264},{12,268},{16,272},{20,276},{24,280},{28,28... | collective-permute-start | bytes 12296 | tf_op jit(solution)/shard_map/ppermute | solution.py:26
  117.6 4.6 %copy-start.14 = (s32[8]{0:T(128)S(1)}, s32[8]{0:T(128)}, u32[]{:S(2)}) copy-start(s32[8]{0:T(128)} %dynamic_slice.98) | copy-start | bytes 100
  220.8 5.2 %copy-start.1 = (f32[32,32,64]{2,0,1:T(8,128)S(1)}, f32[32,32,64]{2,0,1:T(8,128)}, u32[]{:S(2)}) copy-start(f32[32,32,64]{2,0,1:T(8,128)} %convolution_bitcast_fusion.2) | copy-start | bytes 786436
  221.9 13.2 %all-to-all-start = ((bf16[4,32,2048]{2,1,0:T(8,128)(2,1)}), bf16[4,32,2048]{2,1,0:T(8,128)(2,1)}, u32[]{:S(2)}, u32[]{:S(2)}) async-start(bf16[4,32,2048]{2,1,0:T(8,128)(2,1)} %convert_element_type.77), calls=%async_computation | async-start | bytes 1048576 | tf_op jit(solution)/shard_map/all_to_all | solution.py:94
Sparse Core Ops, SparseCore 0:
  63.3 49.6 all-gather.1
where the time goes:
time: 247 us; the launch traced here: 244 us
  local copies, waits for them, and re-layouts  62.7 us (25%)
  matrix products  62.2 us (25%)
  starting transfers between devices  44.3 us (18%)
  waiting for transfers between devices  39.9 us (16%)
  other arithmetic  20.4 us (8%)
  between operations  13.9 us (6%)
    dot_general x12, matrix products, add_slot(): jnp.einsum('rcs,cts->rct', source_values, near_block, preferred_element_t...  50.4 us
    ppermute x7, starting transfers between devices, from_partner(): lax.ppermute(value, axis, [(i, i ^ 1 << apart) for i in range(lax.axis_si...  30.3 us
    gather x12, local copies, waits for them, and re-layouts, add_slot(): source_values = jnp.take(sources, window_index + first_local, axis=1)  28.7 us
    all_gather x1, waiting for transfers between devices, per_device(): sources = lax.all_gather(value_rows, 'rhs', axis=0, tiled=True)  21.3 us
    ppermute x7, waiting for transfers between devices, from_partner(): lax.ppermute(value, axis, [(i, i ^ 1 << apart) for i in range(lax.axis_si...  12.5 us
    reduce_and x12, other arithmetic, add_slot(): source_values = jnp.take(sources, window_index + first_local, axis=1)  8.28 us
    gather x12, local copies, waits for them, and re-layouts, add_slot(): source_geometry = jnp.take(local_geometry, window_index, axis=1)  6.92 us
    all_to_all x1, waiting for transfers between devices, per_device(): lax.all_to_all(near_part.reshape(all_rows, per_part * panels).astype(jnp....  6.04 us
  transfers between devices with their start and end apart: 13, of which 6 were waited for; matrix products, arithmetic and copies ran while one was open for 13% of the time, Pallas kernels for 0%

commit v1 on v0

--- a/solution.py
+++ b/solution.py
@@ -7,6 +7,32 @@
 NNEAR = 12
 NWIN = 6
 FWIN = 8
+
+
+def _form_bench(frame_in, link_axis, k_dim):
+    local_part = lax.axis_size(link_axis)
+    lower, field_out, p_next = (local_part, lax.axis_index(link_axis), frame_in.shape[k_dim])
+    found = tuple((h * lower if t == k_dim else h for t, h in enumerate(frame_in.shape)))
+    back = lax.dynamic_update_slice_in_dim(
+        jnp.zeros(found, frame_in.dtype), frame_in, field_out * p_next, axis=k_dim
+    )
+    u1 = part_now = frame_in
+    for num in [*range(1, lower // 2 + 1)]:
+        carry = tuple(((t, (t + 1) % lower) for t in range(lower)))
+        u1 = lax.ppermute(u1, axis_name=link_axis, perm=carry)
+        back = lax.dynamic_update_slice_in_dim(
+            back, u1, (field_out - num) % lower * p_next, axis=k_dim
+        )
+        if 2 * num < lower:
+            part_now = lax.ppermute(
+                part_now,
+                axis_name=link_axis,
+                perm=tuple(((t, (t - 1) % lower) for t in range(lower))),
+            )
+            back = lax.dynamic_update_slice_in_dim(
+                back, part_now, (field_out + num) % lower * p_next, axis=k_dim
+            )
+    return back
 
 
 def with_halo(value, sides, width):
@@ -66,7 +92,7 @@
     extended = with_halo(stacked, (("leaf", 1),), NWIN * panels)
     wide_rows = extended.shape[1] // panels
     value_rows = extended[:rows_here].astype(jnp.bfloat16)
-    sources = lax.all_gather(value_rows, "rhs", axis=0, tiled=True)
+    sources = _form_bench(value_rows, "rhs", 0)
     sources = sources.reshape(rows_here * column_parts, wide_rows, panels)
     all_rows = sources.shape[0]
     wide_geometry = extended[rows_here:].reshape(4, wide_rows, panels)

time: 247 us -> 369 us (1.49)
  the two profiles are of different devices: /device:TPU:1 before, /device:TPU:56 now
where the time goes in v1:
time: 369 us; the launch traced here: 363 us
  local copies, waits for them, and re-layouts  191 us (52%)
  matrix products  63.3 us (17%)
  starting transfers between devices  58.3 us (16%)
  waiting for transfers between devices  30.3 us (8%)
  other arithmetic  19.3 us (5%)
    dynamic_update_slice x2, local copies, waits for them, and re-layouts, _form_bench(): lax.dynamic_update_slice_in_dim(back, u1, (field_out - num) % lower * p_n...  61.8 us
    dot_general x12, matrix products, add_slot(): jnp.einsum('rcs,cts->rct', source_values, near_block, preferred_element_t...  50.4 us
    ppermute x7, starting transfers between devices, from_partner(): lax.ppermute(value, axis, [(i, i ^ 1 << apart) for i in range(lax.axis_si...  32.2 us
    dynamic_update_slice x1, local copies, waits for them, and re-layouts, _form_bench(): lax.dynamic_update_slice_in_dim(back, part_now, (field_out + num) % lower...  30.9 us
    gather x12, local copies, waits for them, and re-layouts, add_slot(): source_values = jnp.take(sources, window_index + first_local, axis=1)  28.7 us
    dynamic_update_slice x1, local copies, waits for them, and re-layouts, _form_bench(): lax.dynamic_update_slice_in_dim(jnp.zeros(found, frame_in.dtype), frame_i...  26.3 us
    ppermute x7, waiting for transfers between devices, from_partner(): lax.ppermute(value, axis, [(i, i ^ 1 << apart) for i in range(lax.axis_si...  17.1 us
    reduce_and x12, other arithmetic, add_slot(): source_values = jnp.take(sources, window_index + first_local, axis=1)  8.35 us
  transfers between devices with their start and end apart: 15, of which 7 were waited for; matrix products, arithmetic and copies ran while one was open for 35% of the time, Pallas kernels for 0%

profile of v1, /device:TPU:56, one launch (start us, length us, event | category | flops | bytes accessed | tf_op | source)
XLA Modules:
  0.0 363.4 jit_solution(817704173546104913)
XLA Ops:
  2.7 2.8 collective-permute-start.1
  12.7 3.6 collective-permute-start.6
  16.3 3.1 collective-permute-start.5
  20.8 5.8 %collective-permute-start.7 = (bf16[32,64]{1,0:T(8,128)(2,1)S(1)}, bf16[32,64]{1,0:T(8,128)(2,1)S(1)}, u32[]{:S(2)}, u32[]{:S(2)}) collective-permute-start(bf16[32,64]{1,0:T(8,128)(2,1)S(1)} %fusion.23), channel_id=1, source_target_pairs={{0,4},{4,0},{8,12},{12,8},{16,20},{20,16},{24,28},{28,24},{32,36},... | collective-permute-start | bytes 12296 | tf_op jit(solution)/shard_map/ppermute | solution.py:52
  31.1 3.5 collective-permute-done.8
  36.8 4.4 %collective-permute-done.9 = bf16[32,64]{1,0:T(8,128)(2,1)S(1)} collective-permute-done((bf16[32,64]{1,0:T(8,128)(2,1)S(1)}, bf16[32,64]{1,0:T(8,128)(2,1)S(1)}, u32[]{:S(2)}, u32[]{:S(2)}) %collective-permute-start.9) | collective-permute-done | bytes 4128 | tf_op jit(solution)/shard_map/ppermute | solution.py:52
  41.3 3.0 collective-permute-start.10
  44.5 6.3 %collective-permute-done.10 = bf16[32,64]{1,0:T(8,128)(2,1)S(1)} collective-permute-done((bf16[32,64]{1,0:T(8,128)(2,1)S(1)}, bf16[32,64]{1,0:T(8,128)(2,1)S(1)}, u32[]{:S(2)}, u32[]{:S(2)}) %collective-permute-start.10) | collective-permute-done | bytes 4128 | tf_op jit(solution)/shard_map/ppermute | solution.py:52
  50.9 4.3 %collective-permute-start.11 = (bf16[32,64]{1,0:T(8,128)(2,1)S(1)}, bf16[32,64]{1,0:T(8,128)(2,1)S(1)}, u32[]{:S(2)}, u32[]{:S(2)}) collective-permute-start(bf16[32,64]{1,0:T(8,128)(2,1)S(1)} %fusion.27), channel_id=1, source_target_pairs={{0,64},{4,68},{8,72},{12,76},{16,80},{20,84},{24,88},{28,92},{32,9... | collective-permute-start | bytes 12296 | tf_op jit(solution)/shard_map/ppermute | solution.py:52
  56.9 8.5 %collective-permute-start.12 = (bf16[32,64]{1,0:T(8,128)(2,1)S(1)}, bf16[32,64]{1,0:T(8,128)(2,1)S(1)}, u32[]{:S(2)}, u32[]{:S(2)}) collective-permute-start(bf16[32,64]{1,0:T(8,128)(2,1)S(1)} %fusion.28), channel_id=1, source_target_pairs={{0,128},{4,132},{8,136},{12,140},{16,144},{20,148},{24,152},{28,15... | collective-permute-start | bytes 12296 | tf_op jit(solution)/shard_map/ppermute | solution.py:52
  67.8 6.9 %collective-permute-start.13 = (bf16[32,64]{1,0:T(8,128)(2,1)}, bf16[32,64]{1,0:T(8,128)(2,1)S(1)}, u32[]{:S(2)}, u32[]{:S(2)}) collective-permute-start(bf16[32,64]{1,0:T(8,128)(2,1)} %fusion.29), channel_id=1, source_target_pairs={{0,256},{4,260},{8,264},{12,268},{16,272},{20,276},{24,280},{28,28... | collective-permute-start | bytes 12296 | tf_op jit(solution)/shard_map/ppermute | solution.py:52
  84.5 3.4 collective-permute-start.2
  89.2 3.6 %collective-permute-start.3 = (bf16[32,11264]{1,0:T(8,128)(2,1)}, bf16[32,11264]{1,0:T(8,128)(2,1)}, u32[]{:S(2)}, u32[]{:S(2)}) collective-permute-start(bf16[32,11264]{1,0:T(8,128)(2,1)} %slice.115), channel_id=1, source_target_pairs={{0,3},{1,0},{2,1},{3,2},{4,7},{5,4},{6,5},{7,6},{8,11},{9,8},{10,9... | collective-permute-start | bytes 2162696 | tf_op jit(solution)/shard_map/ppermute | solution.py:27
  92.8 8.0 %collective-permute-done.2 = bf16[32,11264]{1,0:T(8,128)(2,1)} collective-permute-done((bf16[32,11264]{1,0:T(8,128)(2,1)}, bf16[32,11264]{1,0:T(8,128)(2,1)}, u32[]{:S(2)}, u32[]{:S(2)}) %collective-permute-start.2) | collective-permute-done | bytes 720928 | tf_op jit(solution)/shard_map/ppermute | solution.py:22
  100.9 3.4 collective-permute-start.4
  108.5 3.8 %copy.59 = bf16[32,11264]{0,1:T(8,128)(2,1)} copy(bf16[32,11264]{1,0:T(8,128)(2,1)} %slice.115) | data formatting | bytes 1441792 | tf_op jit(solution)/shard_map/slice | solution.py:94
  114.3 26.3 %dynamic_update_slice.12 = bf16[128,11264]{0,1:T(8,128)(2,1)} dynamic-update-slice(bf16[128,11264]{0,1:T(8,128)(2,1)} %broadcast_in_dim.64, bf16[32,11264]{0,1:T(8,128)(2,1)} %copy.59, s32[]{:T(128)S(6)} %select_n.206, s32[]{:T(128)} %constant.288.clone.1) | dynamic-update-slice | bytes 1441796 | tf_op jit(solution)/shard_map/dynamic_update_slice | solution.py:16
  140.6 3.8 %copy.60 = bf16[32,11264]{0,1:T(8,128)(2,1)} copy(bf16[32,11264]{1,0:T(8,128)(2,1)} %collective-permute-done.2) | data formatting | bytes 1441792 | tf_op jit(solution)/shard_map/ppermute | solution.py:22
  144.4 30.9 %dynamic_update_slice.13 = bf16[128,11264]{0,1:T(8,128)(2,1)} dynamic-update-slice(bf16[128,11264]{0,1:T(8,128)(2,1)} %dynamic_update_slice.12, bf16[32,11264]{0,1:T(8,128)(2,1)} %copy.60, s32[]{:T(128)S(6)} %select_n.208, s32[]{:T(128)} %constant.288.clone.1) | dynamic-update-slice | bytes 1441796 | tf_op jit(solution)/shard_map/dynamic_update_slice | solution.py:23
  175.3 3.8 %copy.61 = bf16[32,11264]{0,1:T(8,128)(2,1)} copy(bf16[32,11264]{1,0:T(8,128)(2,1)} %collective-permute-done.3) | data formatting | bytes 1441792 | tf_op jit(solution)/shard_map/ppermute | solution.py:27
  179.1 30.9 %dynamic_update_slice.14 = bf16[128,11264]{0,1:T(8,128)(2,1)} dynamic-update-slice(bf16[128,11264]{0,1:T(8,128)(2,1)} %dynamic_update_slice.13, bf16[32,11264]{0,1:T(8,128)(2,1)} %copy.61, s32[]{:T(128)S(6)} %select_n.210, s32[]{:T(128)} %constant.288.clone.1) | dynamic-update-slice | bytes 1441796 | tf_op jit(solution)/shard_map/dynamic_update_slice | solution.py:32
  210.0 3.8 %copy.62 = bf16[32,11264]{0,1:T(8,128)(2,1)} copy(bf16[32,11264]{1,0:T(8,128)(2,1)} %collective-permute-done.4) | data formatting | bytes 1441792 | tf_op jit(solution)/shard_map/ppermute | solution.py:22
  213.8 30.9 %dynamic_update_slice.15 = bf16[128,11264]{0,1:T(8,128)(2,1)} dynamic-update-slice(bf16[128,11264]{0,1:T(8,128)(2,1)} %dynamic_update_slice.14, bf16[32,11264]{0,1:T(8,128)(2,1)} %copy.62, s32[]{:T(128)S(6)} %select_n.212, s32[]{:T(128)} %constant.288.clone.1) | dynamic-update-slice | bytes 1441796 | tf_op jit(solution)/shard_map/dynamic_update_slice | solution.py:23
  244.7 4.5 %copy.64 = bf16[128,44,256]{2,0,1:T(8,128)(2,1)} copy(bf16[128,44,256]{0,2,1:T(8,128)(2,1)} %bitcast.197) | data formatting | bytes 5767168
  249.3 96.8 %while.14 = (s32[]{:T(128)}, f32[128,8,256]{0,2,1:T(8,128)}, s32[8,12]{0,1:T(8,128)}, f32[4,20,256]{2,0,1:T(4,128)S(1)}, f32[4,8,256]{2,1,0:T(8,128)S(1)}, /*ind...) while((s32[]{:T(128)}, f32[128,8,256]{0,2,1:T(8,128)}, ...), condition=%wide.region_1.2_spmd.clone, body=%wide.region_0.1_spmd.clone.sunk | while | flops 142354592 | bytes 4072003 | solution.py:119
  250.7 2.4 gather_fusion.1
  253.1 2.9 fusion.174
  257.5 2.4 gather_fusion.1
  259.9 4.3 %fusion.174 = f32[128,8,256]{0,2,1:T(8,128)} fusion(f32[128,8,256]{0,2,1:T(8,128)} %get-tuple-element.350, f32[8]{0:T(128)S(1)} %compare_convert_fusion.2, f32[8,256]{1,0:T(8,128)S(1)} %get-tuple-element.324, f32[8,256]{1,0:T(8,128)S(1)} %get-tuple-element.328, f32[8,256]{1,0:T(8,128)S(1)} %get-tuple-element.329, ...), kind=kOutput, calls=%fused_computation.6.clone.1 | convolution fusion | flops 142344192 | bytes 2687017 | tf_op jit(solution)/shard_map/while/body/eval_jaxpr/rcs,cts->rct/dot_general | solution.py:114
  265.7 2.4 gather_fusion.1
  268.1 4.3 %fusion.174 = f32[128,8,256]{0,2,1:T(8,128)} fusion(f32[128,8,256]{0,2,1:T(8,128)} %get-tuple-element.350, f32[8]{0:T(128)S(1)} %compare_convert_fusion.2, f32[8,256]{1,0:T(8,128)S(1)} %get-tuple-element.324, f32[8,256]{1,0:T(8,128)S(1)} %get-tuple-element.328, f32[8,256]{1,0:T(8,128)S(1)} %get-tuple-element.329, ...), kind=kOutput, calls=%fused_computation.6.clone.1 | convolution fusion | flops 142344192 | bytes 2687017 | tf_op jit(solution)/shard_map/while/body/eval_jaxpr/rcs,cts->rct/dot_general | solution.py:114
  273.9 2.4 gather_fusion.1
  276.3 4.3 %fusion.174 = f32[128,8,256]{0,2,1:T(8,128)} fusion(f32[128,8,256]{0,2,1:T(8,128)} %get-tuple-element.350, f32[8]{0:T(128)S(1)} %compare_convert_fusion.2, f32[8,256]{1,0:T(8,128)S(1)} %get-tuple-element.324, f32[8,256]{1,0:T(8,128)S(1)} %get-tuple-element.328, f32[8,256]{1,0:T(8,128)S(1)} %get-tuple-element.329, ...), kind=kOutput, calls=%fused_computation.6.clone.1 | convolution fusion | flops 142344192 | bytes 2687017 | tf_op jit(solution)/shard_map/while/body/eval_jaxpr/rcs,cts->rct/dot_general | solution.py:114
  282.1 2.4 gather_fusion.1
  284.5 4.3 %fusion.174 = f32[128,8,256]{0,2,1:T(8,128)} fusion(f32[128,8,256]{0,2,1:T(8,128)} %get-tuple-element.350, f32[8]{0:T(128)S(1)} %compare_convert_fusion.2, f32[8,256]{1,0:T(8,128)S(1)} %get-tuple-element.324, f32[8,256]{1,0:T(8,128)S(1)} %get-tuple-element.328, f32[8,256]{1,0:T(8,128)S(1)} %get-tuple-element.329, ...), kind=kOutput, calls=%fused_computation.6.clone.1 | convolution fusion | flops 142344192 | bytes 2687017 | tf_op jit(solution)/shard_map/while/body/eval_jaxpr/rcs,cts->rct/dot_general | solution.py:114
  292.7 4.3 %fusion.174 = f32[128,8,256]{0,2,1:T(8,128)} fusion(f32[128,8,256]{0,2,1:T(8,128)} %get-tuple-element.350, f32[8]{0:T(128)S(1)} %compare_convert_fusion.2, f32[8,256]{1,0:T(8,128)S(1)} %get-tuple-element.324, f32[8,256]{1,0:T(8,128)S(1)} %get-tuple-element.328, f32[8,256]{1,0:T(8,128)S(1)} %get-tuple-element.329, ...), kind=kOutput, calls=%fused_computation.6.clone.1 | convolution fusion | flops 142344192 | bytes 2687017 | tf_op jit(solution)/shard_map/while/body/eval_jaxpr/rcs,cts->rct/dot_general | solution.py:114
  298.4 2.4 gather_fusion.1
  300.8 4.3 %fusion.174 = f32[128,8,256]{0,2,1:T(8,128)} fusion(f32[128,8,256]{0,2,1:T(8,128)} %get-tuple-element.350, f32[8]{0:T(128)S(1)} %compare_convert_fusion.2, f32[8,256]{1,0:T(8,128)S(1)} %get-tuple-element.324, f32[8,256]{1,0:T(8,128)S(1)} %get-tuple-element.328, f32[8,256]{1,0:T(8,128)S(1)} %get-tuple-element.329, ...), kind=kOutput, calls=%fused_computation.6.clone.1 | convolution fusion | flops 142344192 | bytes 2687017 | tf_op jit(solution)/shard_map/while/body/eval_jaxpr/rcs,cts->rct/dot_general | solution.py:114
  306.6 2.4 gather_fusion.1
  309.0 4.3 %fusion.174 = f32[128,8,256]{0,2,1:T(8,128)} fusion(f32[128,8,256]{0,2,1:T(8,128)} %get-tuple-element.350, f32[8]{0:T(128)S(1)} %compare_convert_fusion.2, f32[8,256]{1,0:T(8,128)S(1)} %get-tuple-element.324, f32[8,256]{1,0:T(8,128)S(1)} %get-tuple-element.328, f32[8,256]{1,0:T(8,128)S(1)} %get-tuple-element.329, ...), kind=kOutput, calls=%fused_computation.6.clone.1 | convolution fusion | flops 142344192 | bytes 2687017 | tf_op jit(solution)/shard_map/while/body/eval_jaxpr/rcs,cts->rct/dot_general | solution.py:114
  314.8 2.4 gather_fusion.1
  317.2 4.3 %fusion.174 = f32[128,8,256]{0,2,1:T(8,128)} fusion(f32[128,8,256]{0,2,1:T(8,128)} %get-tuple-element.350, f32[8]{0:T(128)S(1)} %compare_convert_fusion.2, f32[8,256]{1,0:T(8,128)S(1)} %get-tuple-element.324, f32[8,256]{1,0:T(8,128)S(1)} %get-tuple-element.328, f32[8,256]{1,0:T(8,128)S(1)} %get-tuple-element.329, ...), kind=kOutput, calls=%fused_computation.6.clone.1 | convolution fusion | flops 142344192 | bytes 2687017 | tf_op jit(solution)/shard_map/while/body/eval_jaxpr/rcs,cts->rct/dot_general | solution.py:114
  323.0 2.4 gather_fusion.1
  325.4 4.3 %fusion.174 = f32[128,8,256]{0,2,1:T(8,128)} fusion(f32[128,8,256]{0,2,1:T(8,128)} %get-tuple-element.350, f32[8]{0:T(128)S(1)} %compare_convert_fusion.2, f32[8,256]{1,0:T(8,128)S(1)} %get-tuple-element.324, f32[8,256]{1,0:T(8,128)S(1)} %get-tuple-element.328, f32[8,256]{1,0:T(8,128)S(1)} %get-tuple-element.329, ...), kind=kOutput, calls=%fused_computation.6.clone.1 | convolution fusion | flops 142344192 | bytes 2687017 | tf_op jit(solution)/shard_map/while/body/eval_jaxpr/rcs,cts->rct/dot_general | solution.py:114
  333.6 4.3 %fusion.174 = f32[128,8,256]{0,2,1:T(8,128)} fusion(f32[128,8,256]{0,2,1:T(8,128)} %get-tuple-element.350, f32[8]{0:T(128)S(1)} %compare_convert_fusion.2, f32[8,256]{1,0:T(8,128)S(1)} %get-tuple-element.324, f32[8,256]{1,0:T(8,128)S(1)} %get-tuple-element.328, f32[8,256]{1,0:T(8,128)S(1)} %get-tuple-element.329, ...), kind=kOutput, calls=%fused_computation.6.clone.1 | convolution fusion | flops 142344192 | bytes 2687017 | tf_op jit(solution)/shard_map/while/body/eval_jaxpr/rcs,cts->rct/dot_general | solution.py:114
  341.8 4.3 %fusion.174 = f32[128,8,256]{0,2,1:T(8,128)} fusion(f32[128,8,256]{0,2,1:T(8,128)} %get-tuple-element.350, f32[8]{0:T(128)S(1)} %compare_convert_fusion.2, f32[8,256]{1,0:T(8,128)S(1)} %get-tuple-element.324, f32[8,256]{1,0:T(8,128)S(1)} %get-tuple-element.328, f32[8,256]{1,0:T(8,128)S(1)} %get-tuple-element.329, ...), kind=kOutput, calls=%fused_computation.6.clone.1 | convolution fusion | flops 142344192 | bytes 2687017 | tf_op jit(solution)/shard_map/while/body/eval_jaxpr/rcs,cts->rct/dot_general | solution.py:114
  348.9 4.1 %all-to-all-start = ((bf16[4,32,2048]{2,1,0:T(8,128)(2,1)}), bf16[4,32,2048]{2,1,0:T(8,128)(2,1)}, u32[]{:S(2)}, u32[]{:S(2)}) async-start(bf16[4,32,2048]{2,1,0:T(8,128)(2,1)} %convert_element_type.77), calls=%async_computation | async-start | bytes 1048576 | tf_op jit(solution)/shard_map/all_to_all | solution.py:120
  356.0 5.1 %all-to-all-done = bf16[4,32,2048]{2,1,0:T(8,128)(2,1)} async-done(((bf16[4,32,2048]{2,1,0:T(8,128)(2,1)}), bf16[4,32,2048]{2,1,0:T(8,128)(2,1)}, u32[]{:S(2)}, u32[]{:S(2)}) %all-to-all-start) | async-done | bytes 524320 | tf_op jit(solution)/shard_map/all_to_all | solution.py:120
  (259 shorter events, 71.6 us)
Async XLA Ops:
  0.0 106.3 %copy-start = (bf16[32,4,64,64]{3,2,1,0:T(8,128)(2,1)S(1)}, bf16[32,4,64,64]{3,2,1,0:T(8,128)(2,1)}, u32[]{:S(2)}) copy-start(bf16[32,4,64,64]{3,2,1,0:T(8,128)(2,1)} %param.24) | copy-start | bytes 3145732
  0.0 1.8 copy-start.9
  0.0 7.5 %copy-start.5 = (bf16[32,256,64]{1,2,0:T(8,128)(2,1)S(1)}, bf16[32,256,64]{1,2,0:T(8,128)(2,1)}, u32[]{:S(2)}) copy-start(bf16[32,256,64]{1,2,0:T(8,128)(2,1)} %param.20) | copy-start | bytes 3145732
  2.7 24.0 %copy-start.14 = (s32[32,4]{0,1:T(4,128)S(1)}, s32[32,4]{0,1:T(4,128)}, u32[]{:S(2)}) copy-start(s32[32,4]{0,1:T(4,128)} %param.19) | copy-start | bytes 1540
  2.7 25.3 %copy-start.13 = (s32[32,12]{0,1:T(8,128)S(1)}, s32[32,12]{0,1:T(8,128)}, u32[]{:S(2)}) copy-start(s32[32,12]{0,1:T(8,128)} %param.18) | copy-start | bytes 4612
  2.7 25.9 %copy-start.7 = (bf16[2,64,64]{2,1,0:T(8,128)(2,1)S(1)}, bf16[2,64,64]{2,1,0:T(8,128)(2,1)}, u32[]{:S(2)}) copy-start(bf16[2,64,64]{2,1,0:T(8,128)(2,1)} %param.26) | copy-start | bytes 49156
  2.7 26.1 %copy-start.4 = (bf16[2,64,64]{2,1,0:T(8,128)(2,1)S(1)}, bf16[2,64,64]{2,1,0:T(8,128)(2,1)}, u32[]{:S(2)}) copy-start(bf16[2,64,64]{2,1,0:T(8,128)(2,1)} %param.25) | copy-start | bytes 49156
  2.7 78.4 %collective-permute-start.1 = (f32[36,1536]{1,0:T(8,128)}, f32[36,1536]{1,0:T(8,128)}, u32[]{:S(2)}, u32[]{:S(2)}) collective-permute-start(f32[36,1536]{1,0:T(8,128)} %get-tuple-element.255), channel_id=1, source_target_pairs={{4,0},{8,4},{12,8},{16,12},{20,16},{24,20},{28,24},{32,28},{36,32}... | collective-permute-start | bytes 663560 | tf_op jit(solution)/shard_map/ppermute | solution.py:46
  5.6 75.5 %collective-permute-start = (f32[36,1536]{1,0:T(8,128)}, f32[36,1536]{1,0:T(8,128)}, u32[]{:S(2)}, u32[]{:S(2)}) collective-permute-start(f32[36,1536]{1,0:T(8,128)} %get-tuple-element.254), channel_id=1, source_target_pairs={{0,4},{4,8},{8,12},{12,16},{16,20},{20,24},{24,28},{28,32},{32,36}... | collective-permute-start | bytes 663560 | tf_op jit(solution)/shard_map/ppermute | solution.py:45
  7.5 71.0 %copy-start.8 = (bf16[2,64,64]{2,1,0:T(8,128)(2,1)S(1)}, bf16[2,64,64]{2,1,0:T(8,128)(2,1)}, u32[]{:S(2)}) copy-start(bf16[2,64,64]{2,1,0:T(8,128)(2,1)} %param.27) | copy-start | bytes 49156
  7.9 0.7 copy-start.2
  12.7 91.5 %collective-permute-start.6 = (bf16[32,512]{1,0:T(8,128)(2,1)}, bf16[32,512]{1,0:T(8,128)(2,1)}, u32[]{:S(2)}, u32[]{:S(2)}) collective-permute-start(bf16[32,512]{1,0:T(8,128)(2,1)} %get-tuple-element.259), channel_id=1, source_target_pairs={{4,0},{8,4},{12,8},{16,12},{20,16},{24,20},{28,24},{32,28},{36,32}... | collective-permute-start | bytes 98312 | tf_op jit(solution)/shard_map/ppermute | solution.py:46
  16.3 87.9 %collective-permute-start.5 = (bf16[32,512]{1,0:T(8,128)(2,1)}, bf16[32,512]{1,0:T(8,128)(2,1)}, u32[]{:S(2)}, u32[]{:S(2)}) collective-permute-start(bf16[32,512]{1,0:T(8,128)(2,1)} %get-tuple-element.258), channel_id=1, source_target_pairs={{0,4},{4,8},{8,12},{12,16},{16,20},{20,24},{24,28},{28,32},{32,36}... | collective-permute-start | bytes 98312 | tf_op jit(solution)/shard_map/ppermute | solution.py:45
  20.8 8.1 %collective-permute-start.7 = (bf16[32,64]{1,0:T(8,128)(2,1)S(1)}, bf16[32,64]{1,0:T(8,128)(2,1)S(1)}, u32[]{:S(2)}, u32[]{:S(2)}) collective-permute-start(bf16[32,64]{1,0:T(8,128)(2,1)S(1)} %fusion.23), channel_id=1, source_target_pairs={{0,4},{4,0},{8,12},{12,8},{16,20},{20,16},{24,28},{28,24},{32,36},... | collective-permute-start | bytes 12296 | tf_op jit(solution)/shard_map/ppermute | solution.py:52
  28.9 53.4 %copy-start.10 = (bf16[32,64]{1,0:T(8,128)(2,1)}, bf16[32,64]{1,0:T(8,128)(2,1)S(1)}, u32[]{:S(2)}) copy-start(bf16[32,64]{1,0:T(8,128)(2,1)S(1)} %collective-permute-done.7) | copy-start | bytes 12292
  29.1 5.5 %collective-permute-start.8 = (bf16[32,64]{1,0:T(8,128)(2,1)S(1)}, bf16[32,64]{1,0:T(8,128)(2,1)S(1)}, u32[]{:S(2)}, u32[]{:S(2)}) collective-permute-start(bf16[32,64]{1,0:T(8,128)(2,1)S(1)} %fusion.24), channel_id=1, source_target_pairs={{0,8},{4,12},{8,0},{12,4},{16,24},{20,28},{24,16},{28,20},{32,40},... | collective-permute-start | bytes 12296 | tf_op jit(solution)/shard_map/ppermute | solution.py:52
  34.7 6.4 %collective-permute-start.9 = (bf16[32,64]{1,0:T(8,128)(2,1)S(1)}, bf16[32,64]{1,0:T(8,128)(2,1)S(1)}, u32[]{:S(2)}, u32[]{:S(2)}) collective-permute-start(bf16[32,64]{1,0:T(8,128)(2,1)S(1)} %fusion.25), channel_id=1, source_target_pairs={{0,16},{4,20},{8,24},{12,28},{16,0},{20,4},{24,8},{28,12},{32,48},... | collective-permute-start | bytes 12296 | tf_op jit(solution)/shard_map/ppermute | solution.py:52
  41.3 9.4 %collective-permute-start.10 = (bf16[32,64]{1,0:T(8,128)(2,1)S(1)}, bf16[32,64]{1,0:T(8,128)(2,1)S(1)}, u32[]{:S(2)}, u32[]{:S(2)}) collective-permute-start(bf16[32,64]{1,0:T(8,128)(2,1)S(1)} %fusion.26), channel_id=1, source_target_pairs={{0,32},{4,36},{8,40},{12,44},{16,48},{20,52},{24,56},{28,60},{32,0... | collective-permute-start | bytes 12296 | tf_op jit(solution)/shard_map/ppermute | solution.py:52
  50.9 5.9 %collective-permute-start.11 = (bf16[32,64]{1,0:T(8,128)(2,1)S(1)}, bf16[32,64]{1,0:T(8,128)(2,1)S(1)}, u32[]{:S(2)}, u32[]{:S(2)}) collective-permute-start(bf16[32,64]{1,0:T(8,128)(2,1)S(1)} %fusion.27), channel_id=1, source_target_pairs={{0,64},{4,68},{8,72},{12,76},{16,80},{20,84},{24,88},{28,92},{32,9... | collective-permute-start | bytes 12296 | tf_op jit(solution)/shard_map/ppermute | solution.py:52
  56.8 11.0 %copy-start.11 = (bf16[32,64]{1,0:T(8,128)(2,1)}, bf16[32,64]{1,0:T(8,128)(2,1)S(1)}, u32[]{:S(2)}) copy-start(bf16[32,64]{1,0:T(8,128)(2,1)S(1)} %collective-permute-done.11) | copy-start | bytes 12292
  56.9 10.1 %collective-permute-start.12 = (bf16[32,64]{1,0:T(8,128)(2,1)S(1)}, bf16[32,64]{1,0:T(8,128)(2,1)S(1)}, u32[]{:S(2)}, u32[]{:S(2)}) collective-permute-start(bf16[32,64]{1,0:T(8,128)(2,1)S(1)} %fusion.28), channel_id=1, source_target_pairs={{0,128},{4,132},{8,136},{12,140},{16,144},{20,148},{24,152},{28,15... | collective-permute-start | bytes 12296 | tf_op jit(solution)/shard_map/ppermute | solution.py:52
  67.0 7.6 %copy-start.12 = (bf16[32,64]{1,0:T(8,128)(2,1)}, bf16[32,64]{1,0:T(8,128)(2,1)S(1)}, u32[]{:S(2)}) copy-start(bf16[32,64]{1,0:T(8,128)(2,1)S(1)} %collective-permute-done.12) | copy-start | bytes 12292
  67.8 10.7 %collective-permute-start.13 = (bf16[32,64]{1,0:T(8,128)(2,1)}, bf16[32,64]{1,0:T(8,128)(2,1)S(1)}, u32[]{:S(2)}, u32[]{:S(2)}) collective-permute-start(bf16[32,64]{1,0:T(8,128)(2,1)} %fusion.29), channel_id=1, source_target_pairs={{0,256},{4,260},{8,264},{12,268},{16,272},{20,276},{24,280},{28,28... | collective-permute-start | bytes 12296 | tf_op jit(solution)/shard_map/ppermute | solution.py:52
  81.1 23.2 %copy-start.6 = (bf16[32,2048]{1,0:T(8,128)(2,1)S(1)}, bf16[32,2048]{1,0:T(8,128)(2,1)}, u32[]{:S(2)}) copy-start(bf16[32,2048]{1,0:T(8,128)(2,1)} %reshape.114) | copy-start | bytes 393220
  82.3 1.2 copy-start.1
  84.5 16.3 %collective-permute-start.2 = (bf16[32,11264]{1,0:T(8,128)(2,1)}, bf16[32,11264]{1,0:T(8,128)(2,1)}, u32[]{:S(2)}, u32[]{:S(2)}) collective-permute-start(bf16[32,11264]{1,0:T(8,128)(2,1)} %slice.115), channel_id=1, source_target_pairs={{0,1},{1,2},{2,3},{3,0},{4,5},{5,6},{6,7},{7,4},{8,9},{9,10},{10,1... | collective-permute-start | bytes 2162696 | tf_op jit(solution)/shard_map/ppermute | solution.py:22
  89.2 86.1 %collective-permute-start.3 = (bf16[32,11264]{1,0:T(8,128)(2,1)}, bf16[32,11264]{1,0:T(8,128)(2,1)}, u32[]{:S(2)}, u32[]{:S(2)}) collective-permute-start(bf16[32,11264]{1,0:T(8,128)(2,1)} %slice.115), channel_id=1, source_target_pairs={{0,3},{1,0},{2,1},{3,2},{4,7},{5,4},{6,5},{7,6},{8,11},{9,8},{10,9... | collective-permute-start | bytes 2162696 | tf_op jit(solution)/shard_map/ppermute | solution.py:27
  100.9 109.2 %collective-permute-start.4 = (bf16[32,11264]{1,0:T(8,128)(2,1)}, bf16[32,11264]{1,0:T(8,128)(2,1)}, u32[]{:S(2)}, u32[]{:S(2)}) collective-permute-start(bf16[32,11264]{1,0:T(8,128)(2,1)} %collective-permute-done.2), channel_id=1, source_target_pairs={{0,1},{1,2},{2,3},{3,0},{4,5},{5,6},{6,7},{7,4},{8,9},{9,10},{10,1... | collective-permute-start | bytes 2162696 | tf_op jit(solution)/shard_map/ppermute | solution.py:22
  108.5 3.8 %slice-start = ((f32[36,11264]{1,0:T(8,128)}), f32[4,11264]{1,0:T(4,128)S(1)}, s32[]{:S(2)}) async-start(f32[36,11264]{1,0:T(8,128)} %copy-done.1), calls=%async_computation.1 | async-start | bytes 360448 | tf_op jit(solution)/shard_map/slice | solution.py:98
  244.7 4.6 %copy-start.15 = (s32[8]{0:T(128)S(1)}, s32[8]{0:T(128)}, u32[]{:S(2)}) copy-start(s32[8]{0:T(128)} %dynamic_slice.98) | copy-start | bytes 100
  347.8 5.2 %copy-start.3 = (f32[32,32,64]{2,0,1:T(8,128)S(1)}, f32[32,32,64]{2,0,1:T(8,128)}, u32[]{:S(2)}) copy-start(f32[32,32,64]{2,0,1:T(8,128)} %convolution_bitcast_fusion.2) | copy-start | bytes 786436
  348.9 12.3 %all-to-all-start = ((bf16[4,32,2048]{2,1,0:T(8,128)(2,1)}), bf16[4,32,2048]{2,1,0:T(8,128)(2,1)}, u32[]{:S(2)}, u32[]{:S(2)}) async-start(bf16[4,32,2048]{2,1,0:T(8,128)(2,1)} %convert_element_type.77), calls=%async_computation | async-start | bytes 1048576 | tf_op jit(solution)/shard_map/all_to_all | solution.py:120
